TPU v7x, 32 devices: a whole 2x2x4 slice. The times are simulated.
32 devices in a mesh: fsdp: 4 (over y, core), ctx: 8 (over z, x).
Axes of the slice: x: 2, y: 2, z: 4, core: 2. Of those that a mesh axis runs over, the one named last changes fastest.
Arguments:
- query_proj: bfloat16 [4, 1024, 4096], P('fsdp', 'ctx'), may hold values from -10 to 10
- key_proj: bfloat16 [4, 1024, 4096], P('fsdp', 'ctx'), may hold values from -10 to 10
- value_proj: bfloat16 [4, 1024, 4096], P('fsdp', 'ctx'), may hold values from -12 to 12
- modality: int32 [4, 1024], P('fsdp', 'ctx'), may hold values from 0 to 1, as said below
- out_weight: bfloat16 [2, 4096, 2048], P(None, ('fsdp', 'ctx')), may hold values from -0.09375 to 0.09375
- grad_projected: bfloat16 [4, 1024, 2048], P('fsdp', 'ctx'), may hold values from -6 to 6
Outputs:
- projected: bfloat16 [4, 1024, 2048], P('fsdp', 'ctx')
- grad_query: bfloat16 [4, 1024, 4096], P('fsdp', 'ctx')
- grad_key: bfloat16 [4, 1024, 4096], P('fsdp', 'ctx')
- grad_value: bfloat16 [4, 1024, 4096], P('fsdp', 'ctx')
Inputs may be any that keep to these rules, and one draw needn't show every extreme that they name: `modality`: each sequence holds exactly two image spans of 256 positions each, one starting within the first half and lying in the first half, the other lying in the second half; all other positions are text, so exactly half of each sequence's positions are image.
All inputs are finite; a program needn't handle non-finite values.
Results may differ from a plain program's by a relative error of at most 0.012.
The roundings to bfloat16 on the way count: a program that leaves them out, or rounds other values in their place, can miss the bound.
Values may be sent and summed in bfloat16 or wider, within the bound.
A program may use at most 320 MiB of HBM per device.

v0:
```python
import jax
import jax.numpy as jnp
from jax import lax
from jax.experimental import pallas as pl
from jax.experimental.pallas import tpu as pltpu
from jax.sharding import PartitionSpec as P

HEAD_SIZE = 128


def block_count(length):
    return max(1, min(8, length // 512))


def probabilities(query_block, key_prefix, offset):
    scaling = query_block.shape[-1] ** (-0.5)
    scores = (
        jnp.einsum("hqd,hkd->hqk", query_block, key_prefix, preferred_element_type=jnp.float32)
        * scaling
    )
    query_places = offset + jnp.arange(query_block.shape[1])
    key_places = jnp.arange(key_prefix.shape[1])
    scores = jnp.where(key_places[None, None, :] <= query_places[None, :, None], scores, -jnp.inf)
    highest = jnp.max(scores, axis=-1, keepdims=True)
    raised = jnp.exp(scores - highest)
    return raised / jnp.sum(raised, axis=-1, keepdims=True)


def attend_forward(queries, keys_all, values_all):
    length = queries.shape[1]
    block_rows = length // block_count(length)
    pieces = []
    for block_index in range(length // block_rows):
        offset = block_index * block_rows
        finish = offset + block_rows
        weights = probabilities(queries[:, offset:finish], keys_all[:, :finish], offset).astype(
            jnp.bfloat16
        )
        output = jnp.einsum(
            "hqk,hkd->hqd", weights, values_all[:, :finish], preferred_element_type=jnp.float32
        )
        pieces.append(output.astype(jnp.bfloat16))
    return jnp.concatenate(pieces, axis=1)


def attend_backward(queries, keys_all, values_all, attention, grad_attention):
    length = queries.shape[1]
    block_rows = length // block_count(length)
    scaling = queries.shape[-1] ** (-0.5)
    grad_keys = jnp.zeros(queries.shape, jnp.float32)
    grad_values = jnp.zeros(queries.shape, jnp.float32)
    query_pieces = []
    for block_index in range(length // block_rows):
        offset = block_index * block_rows
        finish = offset + block_rows
        query_block = queries[:, offset:finish]
        weights = probabilities(query_block, keys_all[:, :finish], offset)
        grad_block = grad_attention[:, offset:finish]
        attn_block = attention[:, offset:finish]
        grad_values = grad_values.at[:, :finish].add(
            jnp.einsum(
                "hqk,hqd->hkd",
                weights.astype(jnp.bfloat16),
                grad_block,
                preferred_element_type=jnp.float32,
            )
        )
        grad_weights = jnp.einsum(
            "hqd,hkd->hqk", grad_block, values_all[:, :finish], preferred_element_type=jnp.float32
        )
        row_delta = jnp.sum(
            grad_block.astype(jnp.float32) * attn_block.astype(jnp.float32), axis=-1, keepdims=True
        )
        grad_scores = (weights * (grad_weights - row_delta) * scaling).astype(jnp.bfloat16)
        query_pieces.append(
            jnp.einsum(
                "hqk,hkd->hqd",
                grad_scores,
                keys_all[:, :finish],
                preferred_element_type=jnp.float32,
            ).astype(jnp.bfloat16)
        )
        grad_keys = grad_keys.at[:, :finish].add(
            jnp.einsum("hqk,hqd->hkd", grad_scores, query_block, preferred_element_type=jnp.float32)
        )
    return (
        jnp.concatenate(query_pieces, axis=1),
        grad_keys.astype(jnp.bfloat16),
        grad_values.astype(jnp.bfloat16),
    )


def transposed_product(left, right):
    return lax.dot_general(
        left, right, (((1,), (1,)), ((), ())), preferred_element_type=jnp.float32
    )


def heads_first(flat, length, local_heads):
    return flat.reshape(length, local_heads, HEAD_SIZE).transpose(1, 0, 2)


def heads_last(stacked, length, local_width):
    return stacked.transpose(1, 0, 2).reshape(1, length, local_width)


def per_device_gathered(query_proj, key_proj, value_proj, modality, out_weight, grad_projected):
    context_size = lax.axis_size("ctx")
    row_count = query_proj.shape[1]
    inner_width = query_proj.shape[2]
    length = row_count * context_size
    local_width = inner_width // context_size
    local_heads = local_width // HEAD_SIZE
    head_query, head_key, head_value = (
        lax.all_to_all(query_proj, "ctx", split_axis=2, concat_axis=1, tiled=True),
        lax.all_to_all(key_proj, "ctx", split_axis=2, concat_axis=1, tiled=True),
        lax.all_to_all(value_proj, "ctx", split_axis=2, concat_axis=1, tiled=True),
    )
    head_query = heads_first(head_query, length, local_heads)
    head_key = heads_first(head_key, length, local_heads)
    head_value = heads_first(head_value, length, local_heads)
    attention = attend_forward(head_query, head_key, head_value)
    sending = heads_last(attention, length, local_width)
    attn_rows = lax.all_to_all(sending, "ctx", split_axis=1, concat_axis=2, tiled=True)[0]
    upstream = grad_projected[0]
    weight_piece = lax.all_gather(out_weight, ("fsdp", "ctx"), axis=1, tiled=True)
    text_out = jnp.dot(attn_rows, weight_piece[0], preferred_element_type=jnp.float32)
    image_out = jnp.dot(attn_rows, weight_piece[1], preferred_element_type=jnp.float32)
    text_grad = transposed_product(upstream, weight_piece[0])
    image_grad = transposed_product(upstream, weight_piece[1])
    text_out, image_out, text_grad, image_grad = (text_out, image_out, text_grad, image_grad)
    image_rows = (modality[0] == 1)[:, None]
    projected = jnp.where(image_rows, image_out, text_out).astype(jnp.bfloat16)[None]
    grad_rows = jnp.where(image_rows, image_grad, text_grad).astype(jnp.bfloat16)
    grad_heads = lax.all_to_all(grad_rows[None], "ctx", split_axis=2, concat_axis=1, tiled=True)
    grad_heads = heads_first(grad_heads, length, local_heads)
    grad_q, grad_k, grad_v = attend_backward(
        head_query, head_key, head_value, attention, grad_heads
    )
    grad_query, grad_key, grad_value = (
        lax.all_to_all(
            heads_last(grad_q, length, local_width), "ctx", split_axis=1, concat_axis=2, tiled=True
        ),
        lax.all_to_all(
            heads_last(grad_k, length, local_width), "ctx", split_axis=1, concat_axis=2, tiled=True
        ),
        lax.all_to_all(
            heads_last(grad_v, length, local_width), "ctx", split_axis=1, concat_axis=2, tiled=True
        ),
    )
    return (projected, grad_query, grad_key, grad_value)


def fused_attention_kernel(
    q_ref, k_ref, v_ref, g_ref, a_ref, dq_ref, dk_ref, dv_ref, dk_sum, dv_sum
):
    length = q_ref.shape[0]
    rows = min(256, length)
    scaling = HEAD_SIZE ** (-0.5)
    nt = (((1,), (1,)), ((), ()))
    tn = (((0,), (0,)), ((), ()))
    for block in reversed(range(length // rows)):
        offset = block * rows
        finish = offset + rows
        q = q_ref[offset:finish, :]
        g = g_ref[offset:finish, :]
        k = k_ref[:finish, :]
        v = v_ref[:finish, :]
        scores = lax.dot_general(q, k, nt, preferred_element_type=jnp.float32) * scaling
        places = lax.broadcasted_iota(jnp.int32, scores.shape, 0) + offset
        scores = jnp.where(
            lax.broadcasted_iota(jnp.int32, scores.shape, 1) <= places, scores, -jnp.inf
        )
        raised = jnp.exp(scores - jnp.max(scores, axis=-1, keepdims=True))
        weights = raised * (1.0 / jnp.sum(raised, axis=-1, keepdims=True))
        weights_bf = weights.astype(jnp.bfloat16)
        attention = jnp.dot(weights_bf, v, preferred_element_type=jnp.float32).astype(jnp.bfloat16)
        a_ref[offset:finish, :] = attention
        delta = jnp.sum(
            g.astype(jnp.float32) * attention.astype(jnp.float32), axis=-1, keepdims=True
        )
        grad_weights = lax.dot_general(g, v, nt, preferred_element_type=jnp.float32)
        grad_scores = (weights * (grad_weights - delta) * scaling).astype(jnp.bfloat16)
        dq_ref[offset:finish, :] = jnp.dot(
            grad_scores, k, preferred_element_type=jnp.float32
        ).astype(jnp.bfloat16)
        dk = lax.dot_general(grad_scores, q, tn, preferred_element_type=jnp.float32)
        dv = lax.dot_general(weights_bf, g, tn, preferred_element_type=jnp.float32)
        if finish == length:
            dk_sum[...] = dk
            dv_sum[...] = dv
        else:
            dk_sum[:finish, :] += dk
            dv_sum[:finish, :] += dv
    dk_ref[...] = dk_sum[...].astype(jnp.bfloat16)
    dv_ref[...] = dv_sum[...].astype(jnp.bfloat16)


def fused_attention(q, k, v, g):
    length, width = q.shape
    spec = pl.BlockSpec((length, HEAD_SIZE), lambda h: (0, h))
    return pl.pallas_call(
        fused_attention_kernel,
        grid=(width // HEAD_SIZE,),
        in_specs=[spec] * 4,
        out_specs=[spec] * 4,
        out_shape=[jax.ShapeDtypeStruct(q.shape, jnp.bfloat16)] * 4,
        scratch_shapes=[pltpu.VMEM((length, HEAD_SIZE), jnp.float32)] * 2,
        compiler_params=pltpu.CompilerParams(vmem_limit_bytes=48 * 2**20),
        cost_estimate=pl.CostEstimate(
            flops=9 * length * length * width, bytes_accessed=16 * length * width, transcendentals=0
        ),
    )(q, k, v, g)


def exchange(arrays, kinds, collective_id):
    size, groups = lax.axis_size("ctx"), lax.axis_size("fsdp")
    places = size // 2
    spans = {
        "deal": size, "ctx": size, "chain": size, "fsdp": groups, "line": places, "swap": 2
    }
    count = len(arrays)

    def block_shape(a, kind):
        if kind in ("deal", "line"):
            return a.shape[1:]
        return (a.shape[0], *a.shape[2:]) if kind == "swap" else a.shape

    blocks = [block_shape(a, kind) for a, kind in zip(arrays, kinds)]
    slots = max(size, groups)

    def body(*refs):
        sources, targets, held = refs[:count], refs[count : 2 * count], refs[2 * count : 3 * count]
        send, receive, load, store, up, down, arrive, across, landed = refs[3 * count :]
        ctx, group = lax.axis_index("ctx"), lax.axis_index("fsdp")
        place, side = ctx // 2, ctx % 2
        position = {
            "deal": ctx, "ctx": ctx, "chain": ctx, "fsdp": group, "line": place, "swap": side
        }

        def device(kind, j):
            if kind == "fsdp":
                return {"fsdp": j}
            if kind == "line":
                return {"ctx": j * 2 + side}
            return {"ctx": place * 2 + j} if kind == "swap" else {"ctx": j}

        def block(i, owner):
            if kinds[i] in ("deal", "line"):
                return sources[i].at[owner]
            return sources[i].at[:, owner] if kinds[i] == "swap" else sources[i]

        def remote(source, target, send_sem, receive_sem, device_id):
            return pltpu.make_async_remote_copy(
                src_ref=source,
                dst_ref=target,
                send_sem=send_sem,
                recv_sem=receive_sem,
                device_id=device_id,
                device_id_type=pl.DeviceIdType.MESH,
            )

        own = [
            pltpu.make_async_copy(block(i, position[kinds[i]]), held[i], load.at[i])
            for i in range(count)
        ]
        for copy in own:
            copy.start()
        barrier = pltpu.get_barrier_semaphore()
        greeted = [({"ctx": lax.rem(ctx + step, size)}) for step in range(1, size)]
        if "fsdp" in kinds:
            greeted += [{"fsdp": lax.rem(group + step, groups)} for step in range(1, groups)]
        for peer in greeted:
            pl.semaphore_signal(barrier, 1, device_id=peer, device_id_type=pl.DeviceIdType.MESH)
        pl.semaphore_wait(barrier, len(greeted))

        copies = []

        def spread(i):
            kind = kinds[i]
            for step in range(1, spans[kind]):
                peer = lax.rem(position[kind] + step, spans[kind])
                copy = remote(
                    block(i, peer),
                    targets[i].at[position[kind]],
                    send.at[i, step],
                    receive.at[i, step],
                    device(kind, peer),
                )
                copy.start()
                copies.append(copy)

        def hop(i, origin, first, ahead, sems):
            slot = targets[i].at[origin * 2 + side]
            source = sources[i] if first else slot
            return remote(
                source, slot, sems.at[origin], arrive.at[origin], {"ctx": ahead * 2 + side}
            )

        def cross(i, origin, first):
            slot = targets[i].at[origin * 2 + side]
            source = sources[i] if first else slot
            return remote(
                source, slot, across.at[origin], landed.at[origin], {"ctx": place * 2 + 1 - side}
            )

        def pass_on(i, distance, finish=False):
            first = distance == 0
            act = (lambda c: c.wait_send()) if finish else (lambda c: c.start())
            for sems, sign in ((up, 1), (down, -1)):
                origin = place - sign * distance
                ahead = place + sign
                there = (origin >= 0) & (origin < places)

                @pl.when(there)
                def _():
                    if not first and not finish:
                        hop(i, origin, first, place, sems).wait_recv()

                    @pl.when((ahead >= 0) & (ahead < places))
                    def _():
                        act(hop(i, origin, first, ahead, sems))

                    if not first or sign == 1:
                        act(cross(i, origin, first))

        chain = kinds.index("chain") if "chain" in kinds else None
        rest = [i for i in range(count) if i != chain]
        deals = [i for i in rest if kinds[i] == "deal"]
        if chain is None:
            for i in rest:
                spread(i)
        else:
            pass_on(chain, 0)
            for i in rest:
                if i not in deals:
                    spread(i)
            for turn in range(max(len(deals), places - 1)):
                if turn < len(deals):
                    spread(deals[turn])
                if turn < places - 1:
                    pass_on(chain, turn + 1)
        for i in range(count):
            own[i].wait()
            back = pltpu.make_async_copy(held[i], targets[i].at[position[kinds[i]]], store.at[i])
            back.start()
            own[i] = back
        for copy in own + copies:
            copy.wait()
        if chain is not None:
            for distance in range(places):
                pass_on(chain, distance, finish=True)
            for origin in range(places):
                slot = targets[chain].at[origin * 2 + 1 - side]
                remote(
                    slot, slot, across.at[origin], landed.at[origin], {"ctx": place * 2 + 1 - side}
                ).wait_recv()

    return pl.pallas_call(
        body,
        in_specs=[pl.BlockSpec(memory_space=pl.ANY)] * count,
        out_specs=[pl.BlockSpec(memory_space=pl.ANY)] * count,
        out_shape=[
            jax.ShapeDtypeStruct((spans[kind], *block), a.dtype)
            for a, kind, block in zip(arrays, kinds, blocks)
        ],
        scratch_shapes=[pltpu.VMEM(block, a.dtype) for a, block in zip(arrays, blocks)]
        + [pltpu.SemaphoreType.DMA((count, slots))] * 2
        + [pltpu.SemaphoreType.DMA((count,))] * 2
        + [pltpu.SemaphoreType.DMA((places,))] * 5,
        compiler_params=pltpu.CompilerParams(collective_id=collective_id, has_side_effects=True),
    )(*arrays)


def per_device(query_proj, key_proj, value_proj, modality, out_weight, grad_projected):
    context_size = lax.axis_size("ctx")
    groups = lax.axis_size("fsdp")
    row_count = query_proj.shape[1]
    piece = out_weight.shape[1]
    length = row_count * context_size
    width = groups * piece

    def to_heads(flat):
        return flat[0].reshape(row_count, groups, context_size, piece).transpose(2, 0, 1, 3).reshape(
            context_size, row_count, width
        )

    def to_rows(blocks):
        split = blocks.reshape(context_size, row_count, groups, piece)
        return split.transpose(1, 2, 0, 3).reshape(1, row_count, width * context_size)

    marks = jnp.broadcast_to(modality, (8, row_count))
    weight, upstream, marks, query, key, value = exchange(
        (
            out_weight,
            grad_projected[0],
            marks,
            to_heads(query_proj),
            to_heads(key_proj),
            to_heads(value_proj),
        ),
        ("fsdp", "chain", "ctx", "deal", "deal", "deal"),
        0,
    )
    image = (marks[:, 0, :] == 1).reshape(length, 1)
    upstream = upstream.reshape(length, -1)
    weight = weight.reshape(groups * 2 * piece, -1)
    both = transposed_product(upstream, weight).reshape(length, groups, 2, piece)
    grad_attention = (
        jnp.where(image[:, :, None], both[:, :, 1], both[:, :, 0])
        .reshape(length, width)
        .astype(jnp.bfloat16)
    )
    attention, grad_q, grad_k, grad_v = fused_attention(
        query.reshape(length, width),
        key.reshape(length, width),
        value.reshape(length, width),
        grad_attention,
    )
    spread = attention.reshape(length, groups, piece)
    zero = jnp.zeros_like(spread)
    spread = jnp.stack(
        [jnp.where(image[:, :, None], zero, spread), jnp.where(image[:, :, None], spread, zero)],
        axis=2,
    ).reshape(length, 2 * width)
    partial = jnp.dot(spread, weight, preferred_element_type=jnp.float32).astype(jnp.bfloat16)
    halves, grad_q, grad_k, grad_v = exchange(
        [partial.reshape(context_size // 2, 2, row_count, -1)]
        + [a.reshape(context_size, row_count, -1) for a in (grad_q, grad_k, grad_v)],
        ("swap", "deal", "deal", "deal"),
        1,
    )
    half = jnp.sum(halves.astype(jnp.float32), axis=0).astype(jnp.bfloat16)
    (partial,) = exchange([half], ("line",), 2)
    projected = jnp.sum(partial.astype(jnp.float32), axis=0).astype(jnp.bfloat16)[None]
    return projected, to_rows(grad_q), to_rows(grad_k), to_rows(grad_v)


def aligned(mesh, query_shape, weight_shape):
    devices = mesh.shape["fsdp"] * mesh.shape["ctx"]
    return (weight_shape[1] // devices) % HEAD_SIZE == 0 and query_shape[1] <= 2048 and mesh.shape["ctx"] % 2 == 0


def solution(mesh):
    placed = (
        P("fsdp", "ctx", None),
        P("fsdp", "ctx", None),
        P("fsdp", "ctx", None),
        P("fsdp", "ctx"),
        P(None, ("fsdp", "ctx"), None),
        P("fsdp", "ctx", None),
    )
    def whole(*arrays):
        local = per_device if aligned(mesh, arrays[0].shape, arrays[4].shape) else per_device_gathered
        return jax.shard_map(
            local,
            mesh=mesh,
            in_specs=placed,
            out_specs=(P("fsdp", "ctx", None),) * 4,
            check_vma=False,
        )(*arrays)

    return whole
```

profile of v0, /device:TPU:8, one launch (start us, length us, event | category | flops | bytes accessed | tf_op | source)
XLA Modules:
  0.0 311.5 jit_solution(9941928999920729562)
XLA Ops:
  0.6 0.0 copy-start.4
  0.6 1.3 broadcast_in_dim.33.refs_2_
  2.0 1.4 copy.34
  3.4 0.4 copy.44
  3.8 0.0 copy-start.5
  3.9 1.2 reshape.97.refs_3_
  5.1 0.0 copy-done.4
  5.1 0.2 copy.35
  5.3 0.4 copy.43
  5.7 1.2 reshape.98.refs_4_
  7.0 0.0 copy-done.5
  7.0 0.2 copy.36
  7.2 0.4 copy.42
  7.6 1.2 reshape.99.refs_5_
  8.9 101.1 %shard_map.93 = (bf16[4,2,128,2048]{3,2,1,0:T(8,128)(2,1)}, bf16[8,128,2048]{2,1,0:T(8,128)(2,1)}, s32[8,8,128]{2,1,0:T(8,128)}, bf16[8,128,512]{2,1,0:T(8,128)(...) custom-call(bf16[2,128,2048]{2,1,0:T(8,128)(2,1)} %refs_0_.1, bf16[128,2048]{1,0:T(8,128)(2,1)} %bitcast.75, ...), custom_call_target="tpu_custom_call" | custom-call | tf_op jit(solution)/shard_map/pallas_call | solution.py:359
  110.0 0.8 compare_reduce_fusion
  110.8 8.0 %fusion.5 = bf16[1024,4,2,128]{0,3,2,1:T(8,128)(2,1)S(1)} fusion(bf16[1024,2048,1,1]{1,0,3,2:T(8,128)(2,1)} %bitcast.79, bf16[4,2,128,2048]{3,2,1,0:T(8,128)(2,1)} %get-tuple-element.23), kind=kOutput, calls=%fused_computation.13 | convolution fusion | flops 4294967296 | bytes 10485760 | tf_op jit(solution)/shard_map/dot_general | solution.py:94
  118.8 1.1 fusion.4
  119.9 0.5 copy.33
  120.5 1.5 copy.32
  122.0 1.2 select_convert_fusion.g_ref
  123.2 0.0 copy-done.3
  123.2 18.3 %shard_map.94 = (bf16[1024,512]{1,0:T(8,128)(2,1)S(1)}, bf16[1024,512]{1,0:T(8,128)(2,1)S(1)}, bf16[1024,512]{1,0:T(8,128)(2,1)S(1)}, bf16[1024,512]{1,0:T(8,128)(2,1)S(1)}) custom-call(bf16[1024,512]{1,0:T(8,128)(2,1)S(1)} %bitcast.58, bf16[1024,512]{1,0:T(8,128)(2,1)} %bitcast.80, bf16[1024,512]{1,0:T(8,128)(2,1)} %bitcast.81, ...), custom_call_target="tpu_custom_call" | custom-call | flops 4831838208 | bytes 8388608 | tf_op jit(solution)/shard_map/pallas_call | solution.py:202
  141.4 0.0 copy-start
  141.4 1.0 copy-done
  142.4 1.0 copy-done.1
  143.4 1.0 copy-done.2
  144.3 0.3 reshape.104
  144.6 0.2 broadcast_select_fusion.1
  144.9 7.8 %bitcast_convert_fusion = bf16[1024,2048]{1,0:T(8,128)(2,1)} fusion(bf16[4,2,128,2048]{3,2,1,0:T(8,128)(2,1)} %get-tuple-element.23, bf16[1024,4,1,128]{3,0,2,1:T(8,128)(2,1)S(1)} %get-tuple-element.35, bf16[1024,4,1,128]{3,0,2,1:T(8,128)(2,1)S(1)} %get-tuple-element.34), kind=kOutput, calls=%fused_computation | convolution fusion | flops 4298113024 | bytes 10485760 | tf_op jit(solution)/shard_map/dot_general | solution.py:426
  152.7 93.4 %shard_map.95 = (bf16[2,4,128,2048]{3,2,1,0:T(8,128)(2,1)}, bf16[8,128,512]{2,1,0:T(8,128)(2,1)}, bf16[8,128,512]{2,1,0:T(8,128)(2,1)}, bf16[8,128,512]{2,1,0:T(8,128)(2,1)}) custom-call(bf16[4,2,128,2048]{3,2,1,0:T(8,128)(2,1)} %bitcast.59, bf16[8,128,512]{2,1,0:T(8,128)(2,1)} %bitcast.55, bf16[8,128,512]{2,1,0:T(8,128)(2,1)} %bitcast.56, ...), custom_call_target="tpu_custom_call" | custom-call | tf_op jit(solution)/shard_map/pallas_call | solution.py:359
  246.1 5.1 %reduce_sum.24.refs_0_ = bf16[4,128,2048]{2,1,0:T(8,128)(2,1)} reduce(bf16[2,4,128,2048]{3,2,1,0:T(8,128)(2,1)} %get-tuple-element.28, bf16[]{:T(256)} %constant.6.clone.1), dimensions={0}, to_apply=%region_0.1 | reduce | flops 1048576 | bytes 6291458 | tf_op jit(solution)/shard_map/reduce_sum | solution.py:433
  251.2 48.9 %shard_map.96 = bf16[4,128,2048]{2,1,0:T(8,128)(2,1)} custom-call(bf16[4,128,2048]{2,1,0:T(8,128)(2,1)} %reduce_sum.24.refs_0_), custom_call_target="tpu_custom_call" | custom-call | tf_op jit(solution)/shard_map/pallas_call | solution.py:359
  300.2 0.0 copy-start.7
  300.2 3.0 reduce_sum.25
  303.2 0.0 copy-done.8
  303.2 0.3 reshape.109
  303.5 1.2 copy.27
  304.7 0.0 copy-start.6
  304.7 1.3 reshape.110
  306.0 0.0 copy-done.7
  306.0 0.3 reshape.111
  306.3 1.2 copy.28
  307.5 1.3 reshape.112
  308.8 0.0 copy-done.6
  308.8 0.3 reshape.113
  309.0 1.2 copy.29
  310.3 1.3 reshape.114
  (4 shorter events, 0.0 us)
Async XLA Ops:
  0.6 4.5 %copy-start.4 = (bf16[1,128,4096]{2,1,0:T(8,128)(2,1)S(1)}, bf16[1,128,4096]{2,1,0:T(8,128)(2,1)}, u32[]{:S(2)}) copy-start(bf16[1,128,4096]{2,1,0:T(8,128)(2,1)} %param.7) | copy-start | bytes 3145732
  3.8 3.1 %copy-start.5 = (bf16[1,128,4096]{2,1,0:T(8,128)(2,1)S(1)}, bf16[1,128,4096]{2,1,0:T(8,128)(2,1)}, u32[]{:S(2)}) copy-start(bf16[1,128,4096]{2,1,0:T(8,128)(2,1)} %param.8) | copy-start | bytes 3145732
  119.9 3.2 %copy-start.3 = (bf16[8,128,512]{2,1,0:T(8,128)(2,1)S(1)}, bf16[8,128,512]{2,1,0:T(8,128)(2,1)}, u32[]{:S(2)}) copy-start(bf16[8,128,512]{2,1,0:T(8,128)(2,1)} %get-tuple-element.19) | copy-start | bytes 3145732
  141.4 1.0 copy-start
  142.4 1.0 copy-start.1
  143.4 1.0 copy-start.2
  251.2 52.0 %copy-start.8 = (bf16[8,128,512]{2,1,0:T(8,128)(2,1)S(1)}, bf16[8,128,512]{2,1,0:T(8,128)(2,1)}, u32[]{:S(2)}) copy-start(bf16[8,128,512]{2,1,0:T(8,128)(2,1)} %get-tuple-element.29) | copy-start | bytes 3145732
  300.2 5.8 %copy-start.7 = (bf16[8,128,512]{2,1,0:T(8,128)(2,1)S(1)}, bf16[8,128,512]{2,1,0:T(8,128)(2,1)}, u32[]{:S(2)}) copy-start(bf16[8,128,512]{2,1,0:T(8,128)(2,1)} %get-tuple-element.30) | copy-start | bytes 3145732
  304.7 4.1 %copy-start.6 = (bf16[8,128,512]{2,1,0:T(8,128)(2,1)S(1)}, bf16[8,128,512]{2,1,0:T(8,128)(2,1)}, u32[]{:S(2)}) copy-start(bf16[8,128,512]{2,1,0:T(8,128)(2,1)} %get-tuple-element.31) | copy-start | bytes 3145732
where the time goes:
time: 312 us
  Pallas kernels  262 us (84%)
  local copies, waits for them, and re-layouts  22.8 us (7%)
  matrix products  15.8 us (5%)
  other arithmetic  10.3 us (3%)
    pallas_call x3, Pallas kernels, exchange(): pl.pallas_call(body, in_specs=[pl.BlockSpec(memory_space=pl.ANY)] * count...  244 us
    pallas_call x1, Pallas kernels, fused_attention(): pl.pallas_call(fused_attention_kernel, grid=(width // HEAD_SIZE,), in_spe...  18.3 us
    dot_general x1, matrix products, transposed_product(): lax.dot_general(left, right, (((1,), (1,)), ((), ())), preferred_element_...  7.99 us
    dot_general x1, matrix products, per_device(): jnp.dot(spread, weight, preferred_element_type=jnp.float32)  7.83 us

commit v1 on v0

v1 whole, which is shorter than its diff:
```python
import functools

import jax
import jax.numpy as jnp
from jax import lax
from jax.experimental import pallas as pl
from jax.experimental.pallas import tpu as pltpu
from jax.sharding import PartitionSpec as P

HEAD_SIZE = 128


def block_count(length):
    return max(1, min(8, length // 512))


def probabilities(query_block, key_prefix, offset):
    scaling = query_block.shape[-1] ** (-0.5)
    scores = (
        jnp.einsum("hqd,hkd->hqk", query_block, key_prefix, preferred_element_type=jnp.float32)
        * scaling
    )
    query_places = offset + jnp.arange(query_block.shape[1])
    key_places = jnp.arange(key_prefix.shape[1])
    scores = jnp.where(key_places[None, None, :] <= query_places[None, :, None], scores, -jnp.inf)
    highest = jnp.max(scores, axis=-1, keepdims=True)
    raised = jnp.exp(scores - highest)
    return raised / jnp.sum(raised, axis=-1, keepdims=True)


def attend_forward(queries, keys_all, values_all):
    length = queries.shape[1]
    block_rows = length // block_count(length)
    pieces = []
    for block_index in range(length // block_rows):
        offset = block_index * block_rows
        finish = offset + block_rows
        weights = probabilities(queries[:, offset:finish], keys_all[:, :finish], offset).astype(
            jnp.bfloat16
        )
        output = jnp.einsum(
            "hqk,hkd->hqd", weights, values_all[:, :finish], preferred_element_type=jnp.float32
        )
        pieces.append(output.astype(jnp.bfloat16))
    return jnp.concatenate(pieces, axis=1)


def attend_backward(queries, keys_all, values_all, attention, grad_attention):
    length = queries.shape[1]
    block_rows = length // block_count(length)
    scaling = queries.shape[-1] ** (-0.5)
    grad_keys = jnp.zeros(queries.shape, jnp.float32)
    grad_values = jnp.zeros(queries.shape, jnp.float32)
    query_pieces = []
    for block_index in range(length // block_rows):
        offset = block_index * block_rows
        finish = offset + block_rows
        query_block = queries[:, offset:finish]
        weights = probabilities(query_block, keys_all[:, :finish], offset)
        grad_block = grad_attention[:, offset:finish]
        attn_block = attention[:, offset:finish]
        grad_values = grad_values.at[:, :finish].add(
            jnp.einsum(
                "hqk,hqd->hkd",
                weights.astype(jnp.bfloat16),
                grad_block,
                preferred_element_type=jnp.float32,
            )
        )
        grad_weights = jnp.einsum(
            "hqd,hkd->hqk", grad_block, values_all[:, :finish], preferred_element_type=jnp.float32
        )
        row_delta = jnp.sum(
            grad_block.astype(jnp.float32) * attn_block.astype(jnp.float32), axis=-1, keepdims=True
        )
        grad_scores = (weights * (grad_weights - row_delta) * scaling).astype(jnp.bfloat16)
        query_pieces.append(
            jnp.einsum(
                "hqk,hkd->hqd",
                grad_scores,
                keys_all[:, :finish],
                preferred_element_type=jnp.float32,
            ).astype(jnp.bfloat16)
        )
        grad_keys = grad_keys.at[:, :finish].add(
            jnp.einsum("hqk,hqd->hkd", grad_scores, query_block, preferred_element_type=jnp.float32)
        )
    return (
        jnp.concatenate(query_pieces, axis=1),
        grad_keys.astype(jnp.bfloat16),
        grad_values.astype(jnp.bfloat16),
    )


def transposed_product(left, right):
    return lax.dot_general(
        left, right, (((1,), (1,)), ((), ())), preferred_element_type=jnp.float32
    )


def heads_first(flat, length, local_heads):
    return flat.reshape(length, local_heads, HEAD_SIZE).transpose(1, 0, 2)


def heads_last(stacked, length, local_width):
    return stacked.transpose(1, 0, 2).reshape(1, length, local_width)


def per_device_gathered(query_proj, key_proj, value_proj, modality, out_weight, grad_projected):
    context_size = lax.axis_size("ctx")
    row_count = query_proj.shape[1]
    inner_width = query_proj.shape[2]
    length = row_count * context_size
    local_width = inner_width // context_size
    local_heads = local_width // HEAD_SIZE
    head_query, head_key, head_value = (
        lax.all_to_all(query_proj, "ctx", split_axis=2, concat_axis=1, tiled=True),
        lax.all_to_all(key_proj, "ctx", split_axis=2, concat_axis=1, tiled=True),
        lax.all_to_all(value_proj, "ctx", split_axis=2, concat_axis=1, tiled=True),
    )
    head_query = heads_first(head_query, length, local_heads)
    head_key = heads_first(head_key, length, local_heads)
    head_value = heads_first(head_value, length, local_heads)
    attention = attend_forward(head_query, head_key, head_value)
    sending = heads_last(attention, length, local_width)
    attn_rows = lax.all_to_all(sending, "ctx", split_axis=1, concat_axis=2, tiled=True)[0]
    upstream = grad_projected[0]
    weight_piece = lax.all_gather(out_weight, ("fsdp", "ctx"), axis=1, tiled=True)
    text_out = jnp.dot(attn_rows, weight_piece[0], preferred_element_type=jnp.float32)
    image_out = jnp.dot(attn_rows, weight_piece[1], preferred_element_type=jnp.float32)
    text_grad = transposed_product(upstream, weight_piece[0])
    image_grad = transposed_product(upstream, weight_piece[1])
    text_out, image_out, text_grad, image_grad = (text_out, image_out, text_grad, image_grad)
    image_rows = (modality[0] == 1)[:, None]
    projected = jnp.where(image_rows, image_out, text_out).astype(jnp.bfloat16)[None]
    grad_rows = jnp.where(image_rows, image_grad, text_grad).astype(jnp.bfloat16)
    grad_heads = lax.all_to_all(grad_rows[None], "ctx", split_axis=2, concat_axis=1, tiled=True)
    grad_heads = heads_first(grad_heads, length, local_heads)
    grad_q, grad_k, grad_v = attend_backward(
        head_query, head_key, head_value, attention, grad_heads
    )
    grad_query, grad_key, grad_value = (
        lax.all_to_all(
            heads_last(grad_q, length, local_width), "ctx", split_axis=1, concat_axis=2, tiled=True
        ),
        lax.all_to_all(
            heads_last(grad_k, length, local_width), "ctx", split_axis=1, concat_axis=2, tiled=True
        ),
        lax.all_to_all(
            heads_last(grad_v, length, local_width), "ctx", split_axis=1, concat_axis=2, tiled=True
        ),
    )
    return (projected, grad_query, grad_key, grad_value)


NT = (((1,), (1,)), ((), ()))
TN = (((0,), (0,)), ((), ()))
AHEAD = 4


def middle_kernel(
    groups,
    size,
    q_in, k_in, v_in, w_in, up_in, mark_in,
    proj_out, dq_out, dk_out, dv_out,
    wbuf, kvbuf, qbuf, up, marks, total, gbuf, obuf, dq_buf, dkv_buf, dk_sum, dv_sum,
    part_out, part_in, proj_buf,
    kv_sem, q_sem, lower_sem, rect_sem, w_sem,
    in_send, lower_send, rect_send, dq_send, dkv_send, w_send,
    single, out_sem, part_send, part_sem,
):
    rows = q_in.shape[0]
    levels = size // 2
    steps = groups * levels
    blocks = size // 2
    half = blocks * rows
    scaling = HEAD_SIZE ** (-0.5)
    group, ctx = lax.axis_index("fsdp"), lax.axis_index("ctx")
    place, side = ctx // 2, ctx % 2
    owner_place = levels // 2 - 1 + place // (levels // 2)
    across = (group + 2) % groups
    partner = group + 1 - 2 * (group % 2)
    position = ctx % blocks

    def columns(step, p):
        turn, which = step // groups, step % groups
        source = (2 - turn) + levels * (turn // 3)
        owner = ((group // 2 + which // 2) % 2) * 2 + (group % 2 + which % 2) % 2
        head = owner * size + 2 * source + p
        return pl.ds(pl.multiple_of(head * HEAD_SIZE, HEAD_SIZE), HEAD_SIZE)

    def remote(source, target, send_sem, receive_sem, device):
        return pltpu.make_async_remote_copy(
            src_ref=source,
            dst_ref=target,
            send_sem=send_sem,
            recv_sem=receive_sem,
            device_id=device,
            device_id_type=pl.DeviceIdType.MESH,
        )

    def arrived(ref, sem):
        remote(ref, ref, sem, sem, {"ctx": (ctx + 1) % size}).wait_recv()

    def sent(ref, sem):
        remote(ref, ref, sem, sem, {"ctx": (ctx + 1) % size}).wait_send()

    def deliver(source, target, send_sem, receive_sem, to):
        @pl.when(to == ctx)
        def _():
            pltpu.make_async_copy(source, target, receive_sem).start()

        @pl.when(to != ctx)
        def _():
            remote(source, target, send_sem, receive_sem, {"ctx": to}).start()

    barrier = pltpu.get_barrier_semaphore()
    greeted = [{"ctx": lax.rem(ctx + step, size)} for step in range(1, size)]
    greeted += [{"fsdp": across}, {"fsdp": partner}]
    for peer in greeted:
        pl.semaphore_signal(barrier, 1, device_id=peer, device_id_type=pl.DeviceIdType.MESH)
    pl.semaphore_wait(barrier, len(greeted))

    own_rows = pl.ds(pl.multiple_of(position * rows, rows), rows)
    key_rows = pl.ds(pl.multiple_of(ctx * rows, rows), rows)

    def send_upstream():
        for p in range(2):
            to = owner_place * 2 + p
            deliver(up_in, up.at[own_rows], single.at[0], single.at[1], to)
            deliver(mark_in, marks.at[own_rows], single.at[2], single.at[3], to)

    def send_step(step):
        for p in range(2):
            to, cols = owner_place * 2 + p, columns(step, p)
            deliver(k_in.at[:, cols], kvbuf.at[step, 0, key_rows], in_send.at[step], kv_sem.at[step], to)
            deliver(v_in.at[:, cols], kvbuf.at[step, 1, key_rows], in_send.at[step], kv_sem.at[step], to)
            deliver(q_in.at[:, cols], qbuf.at[step, own_rows], in_send.at[step], q_sem.at[step], to)

    def leaf(lower):
        turn, moment = (2, 2) if lower else (3, 2)
        send_upstream()

        @pl.loop(0, steps)
        def _(step):
            @pl.when(step == moment)
            def _():
                slot = turn * groups
                remote(
                    w_in, wbuf.at[slot], w_send.at[0, 0], w_sem.at[slot],
                    {"ctx": owner_place * 2 + side},
                ).start()

            send_step(step)

        sent(w_in, w_send.at[0, 0])
        sent(up.at[pl.ds(0, 2 * rows)], single.at[0])
        sent(marks.at[pl.ds(0, 2 * rows)], single.at[2])

        @pl.loop(0, steps)
        def _(step):
            sent(kvbuf.at[step, :, pl.ds(0, 3 * rows)], in_send.at[step])

    def compute(step, base):
        both = lax.dot_general(up[...], wbuf[step], NT, preferred_element_type=jnp.float32)
        image = marks[...] > 0.5
        gbuf[...] = jnp.where(image, both[:, HEAD_SIZE:], both[:, :HEAD_SIZE]).astype(jnp.bfloat16)
        span = half // 2
        for block in reversed(range(2)):
            offset = block * span
            finish = base + offset + span
            q = qbuf[step, offset : offset + span, :]
            g = gbuf[offset : offset + span, :]
            k = kvbuf[step, 0, :finish, :]
            v = kvbuf[step, 1, :finish, :]
            scores = lax.dot_general(q, k, NT, preferred_element_type=jnp.float32) * scaling
            places = lax.broadcasted_iota(jnp.int32, scores.shape, 0) + (base + offset)
            scores = jnp.where(
                lax.broadcasted_iota(jnp.int32, scores.shape, 1) <= places, scores, -jnp.inf
            )
            raised = jnp.exp(scores - jnp.max(scores, axis=-1, keepdims=True))
            weights = raised * (1.0 / jnp.sum(raised, axis=-1, keepdims=True))
            weights_bf = weights.astype(jnp.bfloat16)
            attention = jnp.dot(weights_bf, v, preferred_element_type=jnp.float32).astype(
                jnp.bfloat16
            )
            picked = marks[offset : offset + span, :] > 0.5
            zero = jnp.zeros_like(attention)
            obuf[offset : offset + span, :HEAD_SIZE] = jnp.where(picked, zero, attention)
            obuf[offset : offset + span, HEAD_SIZE:] = jnp.where(picked, attention, zero)
            delta = jnp.sum(
                g.astype(jnp.float32) * attention.astype(jnp.float32), axis=-1, keepdims=True
            )
            grad_weights = lax.dot_general(g, v, NT, preferred_element_type=jnp.float32)
            grad_scores = (weights * (grad_weights - delta) * scaling).astype(jnp.bfloat16)
            dq_buf[step, offset : offset + span, :] = jnp.dot(
                grad_scores, k, preferred_element_type=jnp.float32
            ).astype(jnp.bfloat16)
            dk = lax.dot_general(grad_scores, q, TN, preferred_element_type=jnp.float32)
            dv = lax.dot_general(weights_bf, g, TN, preferred_element_type=jnp.float32)
            if block == 1:
                dk_sum[:finish, :] = dk
                dv_sum[:finish, :] = dv
            else:
                dk_sum[:finish, :] += dk
                dv_sum[:finish, :] += dv
        dkv_buf[step, 0, : base + half, :] = dk_sum[: base + half, :].astype(jnp.bfloat16)
        dkv_buf[step, 1, : base + half, :] = dv_sum[: base + half, :].astype(jnp.bfloat16)
        width = total.shape[1]
        piece = min(512, width)
        for start in range(0, width, piece):
            total[:, start : start + piece] += jnp.dot(
                obuf[...], wbuf[step, :, start : start + piece], preferred_element_type=jnp.float32
            )

    def owner(lower):
        base = 0 if lower else half
        first = 0 if lower else blocks
        own_turn = 1 if lower else 0
        middle = {"ctx": (levels - 1 - place) * 2 + side}

        def pass_on(source, turn, beyond):
            remote(
                source, wbuf.at[turn * groups + 2], w_send.at[0, turn],
                w_sem.at[turn * groups + 2], {"fsdp": across},
            ).start()
            remote(
                source, wbuf.at[turn * groups + 1], w_send.at[1, turn],
                w_sem.at[turn * groups + 1], {"fsdp": partner},
            ).start()
            if beyond:
                remote(
                    source, wbuf.at[turn * groups], w_send.at[2, turn],
                    w_sem.at[turn * groups], middle,
                ).start()

        def relay(turn, beyond):
            slot = turn * groups
            arrived(wbuf.at[slot], w_sem.at[slot])
            pass_on(wbuf.at[slot], turn, beyond)

        def forward(step):
            arrived(kvbuf.at[step, :, pl.ds(0, half)], kv_sem.at[step])
            remote(
                kvbuf.at[step, :, pl.ds(0, half)], kvbuf.at[step, :, pl.ds(0, half)],
                lower_send.at[step], lower_sem.at[step], middle,
            ).start()

        def spread(buffer, skip, output, step, send_sem, receive_sem):
            cols = columns(step, side)
            for b in range(blocks):
                deliver(
                    buffer.at[pl.ds(skip + b * rows, rows)], output.at[:, cols],
                    send_sem, receive_sem, first + b,
                )

        def spread_keys(step):
            spread(dkv_buf.at[step, 0], base, dk_out, step, dkv_send.at[step], out_sem.at[2])
            spread(dkv_buf.at[step, 1], base, dv_out, step, dkv_send.at[step], out_sem.at[3])

        def finish_keys(step):
            arrived(dkv_buf.at[step, :, pl.ds(half, half)], rect_sem.at[step])
            for t in range(2):
                dkv_buf[step, t, :half, :] = (
                    dkv_buf[step, t, :half, :].astype(jnp.float32)
                    + dkv_buf[step, t, half:, :].astype(jnp.float32)
                ).astype(jnp.bfloat16)
            spread_keys(step)

        own_slot = wbuf.at[own_turn * groups]
        load = pltpu.make_async_copy(w_in, own_slot, w_sem.at[own_turn * groups])
        load.start()
        pass_on(w_in, own_turn, True)
        send_upstream()

        @pl.loop(0, steps)
        def _(step):
            send_step(step)

        total[...] = jnp.zeros_like(total)
        load.wait()
        if lower:
            forward(0)
            forward(1)
            relay(0, False)
            for step in range(2, AHEAD):
                forward(step)
        else:
            relay(1, False)
        arrived(up, single.at[1])
        arrived(marks, single.at[3])

        @pl.loop(0, steps)
        def _(step):
            if lower:
                @pl.when(step + AHEAD < steps)
                def _():
                    forward(step + AHEAD)

                @pl.when(step == 3)
                def _():
                    relay(2, True)

                @pl.when(step == 8)
                def _():
                    relay(3, False)

            else:
                @pl.when(step == 1)
                def _():
                    relay(3, True)

                @pl.when(step == 7)
                def _():
                    relay(2, False)

            turn, which = step // groups, step % groups

            @pl.when(which == 2)
            def _():
                arrived(wbuf.at[step], w_sem.at[step])
                remote(
                    wbuf.at[step], wbuf.at[step + 1], w_send.at[3, turn], w_sem.at[step + 1],
                    {"fsdp": partner},
                ).start()

            @pl.when(which % 2 == 1)
            def _():
                arrived(wbuf.at[step], w_sem.at[step])

            arrived(qbuf.at[step], q_sem.at[step])
            if not lower:
                arrived(kvbuf.at[step, :, pl.ds(half, half)], kv_sem.at[step])
                arrived(kvbuf.at[step, :, pl.ds(0, half)], lower_sem.at[step])
            compute(step, base)
            spread(dq_buf.at[step], 0, dq_out, step, dq_send.at[step], out_sem.at[1])
            if lower:
                @pl.when(step >= AHEAD)
                def _():
                    finish_keys(step - AHEAD)

            else:
                remote(
                    dkv_buf.at[step, :, pl.ds(0, half)], dkv_buf.at[step, :, pl.ds(half, half)],
                    rect_send.at[step], rect_sem.at[step], middle,
                ).start()
                spread_keys(step)

        leaf_row = 0 if lower else 1
        for b in (leaf_row, 1 - leaf_row):
            for s in range(2):
                @pl.when(side != s)
                def _():
                    start = (2 * b + s) * rows
                    part_out[b] = total[start : start + rows, :].astype(jnp.bfloat16)

            remote(
                part_out.at[b], part_in.at[b], part_send.at[b], part_sem.at[b],
                {"ctx": place * 2 + 1 - side},
            ).start()
        if lower:
            @pl.loop(steps - AHEAD, steps)
            def _(step):
                finish_keys(step)

        for b in (leaf_row, 1 - leaf_row):
            arrived(part_in.at[b], part_sem.at[b])
            for s in range(2):
                @pl.when(side == s)
                def _():
                    start = (2 * b + s) * rows
                    proj_buf[b] = (
                        total[start : start + rows, :] + part_in[b].astype(jnp.float32)
                    ).astype(jnp.bfloat16)

            if b == leaf_row:
                remote(
                    proj_buf.at[b], proj_out, single.at[4], out_sem.at[0],
                    {"ctx": (0 if lower else levels - 1) * 2 + side},
                ).start()
            else:
                pltpu.make_async_copy(proj_buf.at[b], proj_out, out_sem.at[0]).start()
        for b in range(2):
            sent(part_out.at[b], part_send.at[b])
        sent(proj_buf.at[leaf_row], single.at[4])
        sent(up.at[pl.ds(0, rows)], single.at[0])
        sent(marks.at[pl.ds(0, rows)], single.at[2])

        @pl.loop(0, levels)
        def _(turn):
            for kind in (0, 1, 3):
                sent(w_in, w_send.at[kind, turn])

        for turn in (1, 2) if lower else (0, 3):
            sent(w_in, w_send.at[2, turn])

        @pl.loop(0, steps)
        def _(step):
            sent(qbuf.at[step, pl.ds(0, 3 * rows)], in_send.at[step])
            sent(qbuf.at[step, pl.ds(0, 3 * rows)], dq_send.at[step])
            sent(kvbuf.at[step, :, pl.ds(0, 3 * rows)], dkv_send.at[step])
            if lower:
                sent(kvbuf.at[step, :, pl.ds(0, half)], lower_send.at[step])
            else:
                sent(kvbuf.at[step, :, pl.ds(0, half)], rect_send.at[step])

    @pl.when(place == 0)
    def _():
        leaf(True)

    @pl.when(place == levels - 1)
    def _():
        leaf(False)

    @pl.when(place == levels // 2 - 1)
    def _():
        owner(True)

    @pl.when(place == levels // 2)
    def _():
        owner(False)

    for i, output in enumerate((proj_out, dq_out, dk_out, dv_out)):
        arrived(output, out_sem.at[i])


def per_device(query_proj, key_proj, value_proj, modality, out_weight, grad_projected):
    size, groups = lax.axis_size("ctx"), lax.axis_size("fsdp")
    rows, width = query_proj.shape[1:]
    piece, out_width = out_weight.shape[1:]
    steps, half, length = groups * size // 2, rows * size // 2, rows * size
    marks = jnp.broadcast_to(modality[0][:, None], (rows, HEAD_SIZE)).astype(jnp.float32)
    bf, f32, dma = jnp.bfloat16, jnp.float32, pltpu.SemaphoreType.DMA
    results = pl.pallas_call(
        functools.partial(middle_kernel, groups, size),
        in_specs=[pl.BlockSpec(memory_space=pl.ANY)] * 6,
        out_specs=[pl.BlockSpec(memory_space=pl.ANY)] * 4,
        out_shape=[jax.ShapeDtypeStruct((rows, out_width), bf)]
        + [jax.ShapeDtypeStruct((rows, width), bf)] * 3,
        scratch_shapes=[
            pltpu.VMEM((steps, 2 * piece, out_width), bf),
            pltpu.VMEM((steps, 2, length, HEAD_SIZE), bf),
            pltpu.VMEM((steps, half, HEAD_SIZE), bf),
            pltpu.VMEM((half, out_width), bf),
            pltpu.VMEM((half, HEAD_SIZE), f32),
            pltpu.VMEM((half, out_width), f32),
            pltpu.VMEM((half, HEAD_SIZE), bf),
            pltpu.VMEM((half, 2 * HEAD_SIZE), bf),
            pltpu.VMEM((steps, half, HEAD_SIZE), bf),
            pltpu.VMEM((steps, 2, length, HEAD_SIZE), bf),
            pltpu.VMEM((length, HEAD_SIZE), f32),
            pltpu.VMEM((length, HEAD_SIZE), f32),
            pltpu.VMEM((2, rows, out_width), bf),
            pltpu.VMEM((2, rows, out_width), bf),
            pltpu.VMEM((2, rows, out_width), bf),
        ]
        + [dma((steps,))] * 10
        + [dma((4, size // 2)), dma((5,)), dma((4,)), dma((2,)), dma((2,))],
        compiler_params=pltpu.CompilerParams(
            collective_id=0, has_side_effects=True, vmem_limit_bytes=67043328
        ),
    )(
        query_proj[0],
        key_proj[0],
        value_proj[0],
        out_weight.reshape(2 * piece, out_width),
        grad_projected[0],
        marks,
    )
    return tuple(a[None] for a in results)


def aligned(mesh, query_shape, weight_shape):
    groups, size = mesh.shape["fsdp"], mesh.shape["ctx"]
    return (
        groups == 4
        and size == 8
        and weight_shape[1] == groups * size * HEAD_SIZE
        and query_shape[0] == groups
        and query_shape[1] <= 1024
    )


def solution(mesh):
    placed = (
        P("fsdp", "ctx", None),
        P("fsdp", "ctx", None),
        P("fsdp", "ctx", None),
        P("fsdp", "ctx"),
        P(None, ("fsdp", "ctx"), None),
        P("fsdp", "ctx", None),
    )
    def whole(*arrays):
        local = per_device if aligned(mesh, arrays[0].shape, arrays[4].shape) else per_device_gathered
        return jax.shard_map(
            local,
            mesh=mesh,
            in_specs=placed,
            out_specs=(P("fsdp", "ctx", None),) * 4,
            check_vma=False,
        )(*arrays)

    return whole
```

time: 312 us -> 209 us (0.67); the launches traced: 312 us -> 205 us
  Pallas kernels: 262 us -> 196 us
  matrix products: 15.8 us -> 0 us
  local copies, waits for them, and re-layouts: 22.8 us -> 7.51 us
  other arithmetic: 10.3 us -> 0.01 us
    pallas_call x4 -> x1, Pallas kernels: 262 us -> 196 us  [per_device(): pl.pallas_call(functools.partial(middle_kernel, groups, size), in_specs=[...]
    dot_general x2 -> x0, matrix products: 15.8 us -> none  [the longest x1 7.99 us: transposed_product(): lax.dot_general(left, right, (((1,), (1,)), ((), ())), preferred_element_...]
    reshape x10 -> x0, local copies, waits for them, and re-layouts: 8.56 us -> none  [the longest x3 3.82 us: to_rows(): split.transpose(1, 2, 0, 3).reshape(1, row_count, width * context_size)]
    reduce_sum x2 -> x0, other arithmetic: 8.08 us -> none  [the longest x1 5.08 us: per_device(): half = jnp.sum(halves.astype(jnp.float32), axis=0).astype(jnp.bfloat16)]
    transpose x3 -> x0, local copies, waits for them, and re-layouts: 3.66 us -> none  [to_rows(): split.transpose(1, 2, 0, 3).reshape(1, row_count, width * context_size)]
    unnamed x21 -> x12, local copies, waits for them, and re-layouts: 4.86 us -> 6.8 us
where the time goes in v1:
time: 209 us; the launch traced here: 205 us
  Pallas kernels  196 us (94%)
  local copies, waits for them, and re-layouts  7.51 us (4%)
    pallas_call x1, Pallas kernels, per_device(): pl.pallas_call(functools.partial(middle_kernel, groups, size), in_specs=[...  196 us
    unnamed x12, local copies, waits for them, and re-layouts  6.8 us

profile of v1, /device:TPU:8, one launch (start us, length us, event | category | flops | bytes accessed | tf_op | source)
XLA Modules:
  0.0 204.5 jit_solution(10040916068898035149)
XLA Ops:
  0.6 0.0 copy-start.3
  0.6 0.6 copy-done.3
  1.3 0.7 broadcast_in_dim.17.mark_in
  2.0 196.4 %shard_map.93 = (bf16[128,2048]{1,0:T(8,128)(2,1)}, bf16[128,4096]{1,0:T(8,128)(2,1)}, bf16[128,4096]{1,0:T(8,128)(2,1)}, bf16[128,4096]{1,0:T(8,128)(2,1)}) custom-call(bf16[128,4096]{1,0:T(8,128)(2,1)} %bitcast.14, bf16[128,4096]{1,0:T(8,128)(2,1)} %bitcast.15, bf16[128,4096]{1,0:T(8,128)(2,1)} %bitcast.16, bf16[256,2048]{1,0:T(8,128)(2,1)} %bitcast.17, ...), custom_call_target="tpu_custom_call" | custom-call | tf_op jit(solution)/shard_map/pallas_call | solution.py:534
  198.4 0.0 copy-start.2
  198.4 2.0 copy.14
  200.4 0.0 copy-done.2
  200.4 0.0 copy-start.1
  200.4 1.0 copy.15
  201.3 0.6 copy-done.1
  202.0 0.0 copy-start
  202.0 1.0 copy.16
  202.9 0.6 copy-done
  203.6 1.0 copy.17
  (1 shorter events, 0.0 us)
Async XLA Ops:
  0.6 0.7 copy-start.3
  198.4 2.0 copy-start.2
  200.4 1.6 copy-start.1
  202.0 1.6 copy-start

commit v2 on v1

--- a/solution.py
+++ b/solution.py
@@ -156,6 +156,9 @@
 NT = (((1,), (1,)), ((), ()))
 TN = (((0,), (0,)), ((), ()))
 AHEAD = 4
+BEHIND = 2
+LOWER_SPLIT = 6
+CHUNKS = 8
 
 
 def middle_kernel(
@@ -163,9 +166,9 @@
     size,
     q_in, k_in, v_in, w_in, up_in, mark_in,
     proj_out, dq_out, dk_out, dv_out,
-    wbuf, kvbuf, qbuf, up, marks, total, gbuf, obuf, dq_buf, dkv_buf, dk_sum, dv_sum,
+    wbuf, kvbuf, qbuf, up, tags, marks, total, gbuf, obuf, dq_buf, dkv_buf, dk_sum, dv_sum,
     part_out, part_in, proj_buf,
-    kv_sem, q_sem, lower_sem, rect_sem, w_sem,
+    kv_sem, q_sem, lower_sem, rect_sem, w_sem, chunk_sem,
     in_send, lower_send, rect_send, dq_send, dkv_send, w_send,
     single, out_sem, part_send, part_sem,
 ):
@@ -182,9 +185,14 @@
     partner = group + 1 - 2 * (group % 2)
     position = ctx % blocks
 
+    def halves(lower):
+        split = LOWER_SPLIT * rows // 8 if lower else rows // 2
+        return split, pl.ds(0, split), pl.ds(split, rows - split)
+
     def columns(step, p):
         turn, which = step // groups, step % groups
-        source = (2 - turn) + levels * (turn // 3)
+        late = turn // 2
+        source = (1 - late) * (2 - turn) + late * 3 * (3 - turn)
         owner = ((group // 2 + which // 2) % 2) * 2 + (group % 2 + which % 2) % 2
         head = owner * size + 2 * source + p
         return pl.ds(pl.multiple_of(head * HEAD_SIZE, HEAD_SIZE), HEAD_SIZE)
@@ -224,11 +232,15 @@
     own_rows = pl.ds(pl.multiple_of(position * rows, rows), rows)
     key_rows = pl.ds(pl.multiple_of(ctx * rows, rows), rows)
 
+    def piece(chunk):
+        size_of = w_in.shape[0] // CHUNKS
+        return pl.ds(pl.multiple_of(chunk * size_of, size_of), size_of)
+
     def send_upstream():
         for p in range(2):
             to = owner_place * 2 + p
             deliver(up_in, up.at[own_rows], single.at[0], single.at[1], to)
-            deliver(mark_in, marks.at[own_rows], single.at[2], single.at[3], to)
+            deliver(mark_in, tags.at[position], single.at[2], single.at[3], to)
 
     def send_step(step):
         for p in range(2):
@@ -238,39 +250,58 @@
             deliver(q_in.at[:, cols], qbuf.at[step, own_rows], in_send.at[step], q_sem.at[step], to)
 
     def leaf(lower):
-        turn, moment = (2, 2) if lower else (3, 2)
-        send_upstream()
+        split, first_rows, rest = halves(lower)
+        turn, opening = (3, 4) if lower else (2, 1)
+
+        def send_piece(chunk):
+            remote(
+                w_in.at[piece(chunk)], wbuf.at[turn * groups, piece(chunk)],
+                w_send.at[0, 0], chunk_sem.at[turn, chunk],
+                {"ctx": owner_place * 2 + side},
+            ).start()
+
+        if not lower:
+            @pl.loop(0, CHUNKS)
+            def _(chunk):
+                send_piece(chunk)
 
         @pl.loop(0, steps)
         def _(step):
-            @pl.when(step == moment)
+            @pl.when(step == opening)
             def _():
-                slot = turn * groups
-                remote(
-                    w_in, wbuf.at[slot], w_send.at[0, 0], w_sem.at[slot],
-                    {"ctx": owner_place * 2 + side},
-                ).start()
+                send_upstream()
+
+            if lower:
+                @pl.when((step >= 1) & (step <= CHUNKS))
+                def _():
+                    send_piece(step - 1)
 
             send_step(step)
 
+        arrived(part_in.at[1, rest], part_sem.at[1])
+        arrived(part_in.at[2, rest], part_sem.at[2])
+        proj_buf[0, rest] = (
+            part_in[1, rest].astype(jnp.float32) + part_in[2, rest].astype(jnp.float32)
+        ).astype(jnp.bfloat16)
+        pltpu.make_async_copy(proj_buf.at[0, rest], proj_out.at[rest], out_sem.at[0]).start()
         sent(w_in, w_send.at[0, 0])
         sent(up.at[pl.ds(0, 2 * rows)], single.at[0])
-        sent(marks.at[pl.ds(0, 2 * rows)], single.at[2])
+        sent(tags.at[pl.ds(0, 2)], single.at[2])
 
         @pl.loop(0, steps)
         def _(step):
             sent(kvbuf.at[step, :, pl.ds(0, 3 * rows)], in_send.at[step])
 
-    def compute(step, base):
+    def compute(step, base, between=None):
         both = lax.dot_general(up[...], wbuf[step], NT, preferred_element_type=jnp.float32)
         image = marks[...] > 0.5
         gbuf[...] = jnp.where(image, both[:, HEAD_SIZE:], both[:, :HEAD_SIZE]).astype(jnp.bfloat16)
         span = half // 2
-        for block in reversed(range(2)):
+        kept = []
+        for block in range(2):
             offset = block * span
             finish = base + offset + span
             q = qbuf[step, offset : offset + span, :]
-            g = gbuf[offset : offset + span, :]
             k = kvbuf[step, 0, :finish, :]
             v = kvbuf[step, 1, :finish, :]
             scores = lax.dot_general(q, k, NT, preferred_element_type=jnp.float32) * scaling
@@ -280,14 +311,30 @@
             )
             raised = jnp.exp(scores - jnp.max(scores, axis=-1, keepdims=True))
             weights = raised * (1.0 / jnp.sum(raised, axis=-1, keepdims=True))
-            weights_bf = weights.astype(jnp.bfloat16)
-            attention = jnp.dot(weights_bf, v, preferred_element_type=jnp.float32).astype(
-                jnp.bfloat16
-            )
+            attention = jnp.dot(
+                weights.astype(jnp.bfloat16), v, preferred_element_type=jnp.float32
+            ).astype(jnp.bfloat16)
             picked = marks[offset : offset + span, :] > 0.5
             zero = jnp.zeros_like(attention)
             obuf[offset : offset + span, :HEAD_SIZE] = jnp.where(picked, zero, attention)
             obuf[offset : offset + span, HEAD_SIZE:] = jnp.where(picked, attention, zero)
+            kept.append((weights, attention))
+        width = total.shape[1]
+        wide = min(512, width)
+        for start in range(0, width, wide):
+            total[:, start : start + wide] += jnp.dot(
+                obuf[...], wbuf[step, :, start : start + wide], preferred_element_type=jnp.float32
+            )
+        if between is not None:
+            between()
+        for block in reversed(range(2)):
+            offset = block * span
+            finish = base + offset + span
+            q = qbuf[step, offset : offset + span, :]
+            g = gbuf[offset : offset + span, :]
+            k = kvbuf[step, 0, :finish, :]
+            v = kvbuf[step, 1, :finish, :]
+            weights, attention = kept[block]
             delta = jnp.sum(
                 g.astype(jnp.float32) * attention.astype(jnp.float32), axis=-1, keepdims=True
             )
@@ -297,7 +344,9 @@
                 grad_scores, k, preferred_element_type=jnp.float32
             ).astype(jnp.bfloat16)
             dk = lax.dot_general(grad_scores, q, TN, preferred_element_type=jnp.float32)
-            dv = lax.dot_general(weights_bf, g, TN, preferred_element_type=jnp.float32)
+            dv = lax.dot_general(
+                weights.astype(jnp.bfloat16), g, TN, preferred_element_type=jnp.float32
+            )
             if block == 1:
                 dk_sum[:finish, :] = dk
                 dv_sum[:finish, :] = dv
@@ -306,12 +355,6 @@
                 dv_sum[:finish, :] += dv
         dkv_buf[step, 0, : base + half, :] = dk_sum[: base + half, :].astype(jnp.bfloat16)
         dkv_buf[step, 1, : base + half, :] = dv_sum[: base + half, :].astype(jnp.bfloat16)
-        width = total.shape[1]
-        piece = min(512, width)
-        for start in range(0, width, piece):
-            total[:, start : start + piece] += jnp.dot(
-                obuf[...], wbuf[step, :, start : start + piece], preferred_element_type=jnp.float32
-            )
 
     def owner(lower):
         base = 0 if lower else half
@@ -319,25 +362,26 @@
         own_turn = 1 if lower else 0
         middle = {"ctx": (levels - 1 - place) * 2 + side}
 
-        def pass_on(source, turn, beyond):
+        def pass_on(source, turn, part, beyond):
+            slot = turn * groups
             remote(
-                source, wbuf.at[turn * groups + 2], w_send.at[0, turn],
-                w_sem.at[turn * groups + 2], {"fsdp": across},
+                source, wbuf.at[slot + 2, part], w_send.at[0, turn], w_sem.at[slot + 2],
+                {"fsdp": across},
             ).start()
             remote(
-                source, wbuf.at[turn * groups + 1], w_send.at[1, turn],
-                w_sem.at[turn * groups + 1], {"fsdp": partner},
+                source, wbuf.at[slot + 1, part], w_send.at[1, turn], w_sem.at[slot + 1],
+                {"fsdp": partner},
             ).start()
-            if beyond:
+            if beyond is not None:
                 remote(
-                    source, wbuf.at[turn * groups], w_send.at[2, turn],
-                    w_sem.at[turn * groups], middle,
+                    source, wbuf.at[slot, part], w_send.at[2, turn], beyond, middle,
                 ).start()
 
-        def relay(turn, beyond):
-            slot = turn * groups
-            arrived(wbuf.at[slot], w_sem.at[slot])
-            pass_on(wbuf.at[slot], turn, beyond)
+        def relay(turn, chunk, beyond):
+            part = piece(chunk)
+            source = wbuf.at[turn * groups, part]
+            arrived(source, chunk_sem.at[turn, chunk])
+            pass_on(source, turn, part, chunk_sem.at[turn, chunk] if beyond else None)
 
         def forward(step):
             arrived(kvbuf.at[step, :, pl.ds(0, half)], kv_sem.at[step])
@@ -345,6 +389,10 @@
                 kvbuf.at[step, :, pl.ds(0, half)], kvbuf.at[step, :, pl.ds(0, half)],
                 lower_send.at[step], lower_sem.at[step], middle,
             ).start()
+
+            @pl.when((step >= 1) & (step <= CHUNKS))
+            def _():
+                relay(3, step - 1, True)
 
         def spread(buffer, skip, output, step, send_sem, receive_sem):
             cols = columns(step, side)
@@ -370,7 +418,12 @@
         own_slot = wbuf.at[own_turn * groups]
         load = pltpu.make_async_copy(w_in, own_slot, w_sem.at[own_turn * groups])
         load.start()
-        pass_on(w_in, own_turn, True)
+
+        @pl.loop(0, CHUNKS)
+        def _(chunk):
+            part = piece(chunk)
+            pass_on(w_in.at[part], own_turn, part, chunk_sem.at[own_turn, chunk])
+
         send_upstream()
 
         @pl.loop(0, steps)
@@ -379,40 +432,35 @@
 
         total[...] = jnp.zeros_like(total)
         load.wait()
+
+        @pl.loop(0, CHUNKS)
+        def _(chunk):
+            relay(1 - own_turn, chunk, False)
+            if not lower:
+                relay(2, chunk, True)
+
         if lower:
-            forward(0)
-            forward(1)
-            relay(0, False)
-            for step in range(2, AHEAD):
+            @pl.loop(0, AHEAD)
+            def _(step):
                 forward(step)
-        else:
-            relay(1, False)
+
         arrived(up, single.at[1])
-        arrived(marks, single.at[3])
-
-        @pl.loop(0, steps)
-        def _(step):
+        arrived(tags, single.at[3])
+        for b in range(blocks):
+            wide = jnp.broadcast_to(tags[b].astype(jnp.float32), (HEAD_SIZE, rows))
+            marks[b * rows : (b + 1) * rows, :] = wide.T
+
+        def advance(step, between=None):
             if lower:
                 @pl.when(step + AHEAD < steps)
                 def _():
                     forward(step + AHEAD)
 
-                @pl.when(step == 3)
-                def _():
-                    relay(2, True)
-
-                @pl.when(step == 8)
-                def _():
-                    relay(3, False)
-
-            else:
                 @pl.when(step == 1)
                 def _():
-                    relay(3, True)
-
-                @pl.when(step == 7)
-                def _():
-                    relay(2, False)
+                    @pl.loop(0, CHUNKS)
+                    def _(chunk):
+                        relay(2, chunk, False)
 
             turn, which = step // groups, step % groups
 
@@ -432,12 +480,17 @@
             if not lower:
                 arrived(kvbuf.at[step, :, pl.ds(half, half)], kv_sem.at[step])
                 arrived(kvbuf.at[step, :, pl.ds(0, half)], lower_sem.at[step])
-            compute(step, base)
+
+                @pl.when((step >= 2) & (step < 2 + CHUNKS))
+                def _():
+                    relay(3, step - 2, False)
+
+            compute(step, base, between)
             spread(dq_buf.at[step], 0, dq_out, step, dq_send.at[step], out_sem.at[1])
             if lower:
-                @pl.when(step >= AHEAD)
+                @pl.when(step >= BEHIND)
                 def _():
-                    finish_keys(step - AHEAD)
+                    finish_keys(step - BEHIND)
 
             else:
                 remote(
@@ -446,52 +499,100 @@
                 ).start()
                 spread_keys(step)
 
+        split, first_rows, rest = halves(lower)
         leaf_row = 0 if lower else 1
-        for b in (leaf_row, 1 - leaf_row):
+        near_row = 1 - leaf_row
+        end_place = 0 if lower else levels - 1
+        other = {"ctx": place * 2 + 1 - side}
+
+        def exchange_parts():
             for s in range(2):
                 @pl.when(side != s)
                 def _():
-                    start = (2 * b + s) * rows
-                    part_out[b] = total[start : start + rows, :].astype(jnp.bfloat16)
+                    start = (2 * leaf_row + s) * rows
+                    part_out[0] = total[start : start + rows, :].astype(jnp.bfloat16)
+
+                @pl.when(side == s)
+                def _():
+                    start = (2 * leaf_row + s) * rows + split
+                    part_out[2, rest] = total[start : start + rows - split, :].astype(
+                        jnp.bfloat16
+                    )
 
             remote(
-                part_out.at[b], part_in.at[b], part_send.at[b], part_sem.at[b],
-                {"ctx": place * 2 + 1 - side},
+                part_out.at[0, rest], part_in.at[1, rest], part_send.at[1], part_sem.at[1],
+                {"ctx": end_place * 2 + 1 - side},
             ).start()
+            remote(
+                part_out.at[0, first_rows], part_in.at[0, first_rows], part_send.at[0],
+                part_sem.at[0], other,
+            ).start()
+            remote(
+                part_out.at[2, rest], part_in.at[2, rest], part_send.at[2], part_sem.at[2],
+                {"ctx": end_place * 2 + side},
+            ).start()
+            for s in range(2):
+                @pl.when(side != s)
+                def _():
+                    start = (2 * near_row + s) * rows
+                    part_out[1] = total[start : start + rows, :].astype(jnp.bfloat16)
+
+            remote(
+                part_out.at[1], part_in.at[1], part_send.at[3], part_sem.at[3], other
+            ).start()
+
+        @pl.loop(0, steps - 1)
+        def _(step):
+            advance(step)
+
+        advance(steps - 1, exchange_parts)
         if lower:
-            @pl.loop(steps - AHEAD, steps)
+            @pl.loop(steps - BEHIND, steps - 2)
             def _(step):
                 finish_keys(step)
 
-        for b in (leaf_row, 1 - leaf_row):
-            arrived(part_in.at[b], part_sem.at[b])
-            for s in range(2):
-                @pl.when(side == s)
-                def _():
-                    start = (2 * b + s) * rows
-                    proj_buf[b] = (
-                        total[start : start + rows, :] + part_in[b].astype(jnp.float32)
-                    ).astype(jnp.bfloat16)
-
-            if b == leaf_row:
-                remote(
-                    proj_buf.at[b], proj_out, single.at[4], out_sem.at[0],
-                    {"ctx": (0 if lower else levels - 1) * 2 + side},
-                ).start()
-            else:
-                pltpu.make_async_copy(proj_buf.at[b], proj_out, out_sem.at[0]).start()
-        for b in range(2):
-            sent(part_out.at[b], part_send.at[b])
-        sent(proj_buf.at[leaf_row], single.at[4])
+        arrived(part_in.at[0, first_rows], part_sem.at[0])
+        for s in range(2):
+            @pl.when(side == s)
+            def _():
+                start = (2 * leaf_row + s) * rows
+                proj_buf[0, first_rows] = (
+                    total[start : start + split, :] + part_in[0, first_rows].astype(jnp.float32)
+                ).astype(jnp.bfloat16)
+
+        remote(
+            proj_buf.at[0, first_rows], proj_out.at[first_rows], single.at[4], out_sem.at[0],
+            {"ctx": end_place * 2 + side},
+        ).start()
+        if lower:
+            @pl.loop(steps - 2, steps)
+            def _(step):
+                finish_keys(step)
+
+        arrived(part_in.at[1], part_sem.at[3])
+        for s in range(2):
+            @pl.when(side == s)
+            def _():
+                start = (2 * near_row + s) * rows
+                proj_buf[1] = (
+                    total[start : start + rows, :] + part_in[1].astype(jnp.float32)
+                ).astype(jnp.bfloat16)
+
+        pltpu.make_async_copy(proj_buf.at[1], proj_out, out_sem.at[0]).start()
+        sent(part_out.at[0, first_rows], part_send.at[0])
+        sent(part_out.at[0, rest], part_send.at[1])
+        sent(part_out.at[0, rest], part_send.at[2])
+        sent(part_out.at[1], part_send.at[3])
+        sent(proj_buf.at[0, first_rows], single.at[4])
         sent(up.at[pl.ds(0, rows)], single.at[0])
-        sent(marks.at[pl.ds(0, rows)], single.at[2])
+        sent(tags.at[pl.ds(0, 1)], single.at[2])
 
         @pl.loop(0, levels)
         def _(turn):
             for kind in (0, 1, 3):
                 sent(w_in, w_send.at[kind, turn])
 
-        for turn in (1, 2) if lower else (0, 3):
+        for turn in (1, 3) if lower else (0, 2):
             sent(w_in, w_send.at[2, turn])
 
         @pl.loop(0, steps)
@@ -529,7 +630,6 @@
     rows, width = query_proj.shape[1:]
     piece, out_width = out_weight.shape[1:]
     steps, half, length = groups * size // 2, rows * size // 2, rows * size
-    marks = jnp.broadcast_to(modality[0][:, None], (rows, HEAD_SIZE)).astype(jnp.float32)
     bf, f32, dma = jnp.bfloat16, jnp.float32, pltpu.SemaphoreType.DMA
     results = pl.pallas_call(
         functools.partial(middle_kernel, groups, size),
@@ -542,6 +642,7 @@
             pltpu.VMEM((steps, 2, length, HEAD_SIZE), bf),
             pltpu.VMEM((steps, half, HEAD_SIZE), bf),
             pltpu.VMEM((half, out_width), bf),
+            pltpu.VMEM((size // 2, 1, rows), jnp.int32),
             pltpu.VMEM((half, HEAD_SIZE), f32),
             pltpu.VMEM((half, out_width), f32),
             pltpu.VMEM((half, HEAD_SIZE), bf),
@@ -550,12 +651,14 @@
             pltpu.VMEM((steps, 2, length, HEAD_SIZE), bf),
             pltpu.VMEM((length, HEAD_SIZE), f32),
             pltpu.VMEM((length, HEAD_SIZE), f32),
-            pltpu.VMEM((2, rows, out_width), bf),
-            pltpu.VMEM((2, rows, out_width), bf),
+            pltpu.VMEM((3, rows, out_width), bf),
+            pltpu.VMEM((3, rows, out_width), bf),
             pltpu.VMEM((2, rows, out_width), bf),
         ]
-        + [dma((steps,))] * 10
-        + [dma((4, size // 2)), dma((5,)), dma((4,)), dma((2,)), dma((2,))],
+        + [dma((steps,))] * 5
+        + [dma((size // 2, CHUNKS))]
+        + [dma((steps,))] * 5
+        + [dma((4, size // 2)), dma((5,)), dma((4,)), dma((4,)), dma((4,))],
         compiler_params=pltpu.CompilerParams(
             collective_id=0, has_side_effects=True, vmem_limit_bytes=67043328
         ),
@@ -565,7 +668,7 @@
         value_proj[0],
         out_weight.reshape(2 * piece, out_width),
         grad_projected[0],
-        marks,
+        modality,
     )
     return tuple(a[None] for a in results)
 

time: 209 us -> 175 us (0.84); the launches traced: 205 us -> 173 us
  Pallas kernels: 196 us -> 166 us
    pallas_call x1, Pallas kernels: 196 us -> 166 us  [per_device(): pl.pallas_call(functools.partial(middle_kernel, groups, size), in_specs=[...]
    unnamed x12 -> x10, local copies, waits for them, and re-layouts: 6.8 us -> 6.15 us
where the time goes in v2:
time: 175 us; the launch traced here: 173 us
  Pallas kernels  166 us (95%)
  local copies, waits for them, and re-layouts  6.15 us (4%)
    pallas_call x1, Pallas kernels, per_device(): pl.pallas_call(functools.partial(middle_kernel, groups, size), in_specs=[...  166 us
    unnamed x10, local copies, waits for them, and re-layouts  6.15 us

profile of v2, /device:TPU:8, one launch (start us, length us, event | category | flops | bytes accessed | tf_op | source)
XLA Modules:
  0.0 172.7 jit_solution(12973857182324745019)
XLA Ops:
  0.6 165.9 %shard_map.93 = (bf16[128,2048]{1,0:T(8,128)(2,1)}, bf16[128,4096]{1,0:T(8,128)(2,1)}, bf16[128,4096]{1,0:T(8,128)(2,1)}, bf16[128,4096]{1,0:T(8,128)(2,1)}) custom-call(bf16[128,4096]{1,0:T(8,128)(2,1)} %bitcast.9, bf16[128,4096]{1,0:T(8,128)(2,1)} %bitcast.10, bf16[128,4096]{1,0:T(8,128)(2,1)} %bitcast.11, bf16[256,2048]{1,0:T(8,128)(2,1)} %bitcast.12, ...), custom_call_target="tpu_custom_call" | custom-call | tf_op jit(solution)/shard_map/pallas_call | solution.py:634
  166.5 0.0 copy-start.2
  166.5 2.0 %copy.14 = bf16[1,128,2048]{2,1,0:T(8,128)(2,1)} copy(bf16[1,128,2048]{2,1,0:T(8,128)(2,1)} %bitcast.17) | data formatting | bytes 1048576
  168.5 0.0 copy-done.2
  168.5 0.0 copy-start.1
  168.5 1.0 copy.15
  169.5 0.6 copy-done.1
  170.1 0.0 copy-start
  170.1 1.0 copy.16
  171.1 0.6 copy-done
  171.7 1.0 copy.17
Async XLA Ops:
  166.5 2.0 %copy-start.2 = (bf16[128,4096]{1,0:T(8,128)(2,1)S(1)}, bf16[128,4096]{1,0:T(8,128)(2,1)}, u32[]{:S(2)}) copy-start(bf16[128,4096]{1,0:T(8,128)(2,1)} %get-tuple-element.9) | copy-start | bytes 3145732
  168.5 1.6 copy-start.1
  170.1 1.6 copy-start

commit v3 on v2

--- a/solution.py
+++ b/solution.py
@@ -157,8 +157,9 @@
 TN = (((0,), (0,)), ((), ()))
 AHEAD = 4
 BEHIND = 2
-LOWER_SPLIT = 6
+LOWER_SPLIT, UPPER_SPLIT = 6, 5
 CHUNKS = 8
+PARTS = 4
 
 
 def middle_kernel(
@@ -186,7 +187,7 @@
     position = ctx % blocks
 
     def halves(lower):
-        split = LOWER_SPLIT * rows // 8 if lower else rows // 2
+        split = (LOWER_SPLIT if lower else UPPER_SPLIT) * rows // 8
         return split, pl.ds(0, split), pl.ds(split, rows - split)
 
     def columns(step, p):
@@ -625,6 +626,41 @@
         arrived(output, out_sem.at[i])
 
 
+def settle_kernel(*refs):
+    sources, targets, held, loads, stores = refs[:4], refs[4:8], refs[8:12], refs[12], refs[13]
+    pieces = [(i, h) for i in range(4) for h in range(PARTS)]
+
+    def part(ref, h):
+        count = ref.shape[0] // PARTS
+        return ref.at[pl.ds(h * count, count)]
+
+    def load(i, h):
+        return pltpu.make_async_copy(part(sources[i], h), part(held[i], h), loads.at[i, h])
+
+    def store(i, h):
+        return pltpu.make_async_copy(part(held[i], h), part(targets[i], h), stores.at[i, h])
+
+    for i, h in pieces:
+        load(i, h).start()
+    for i, h in pieces:
+        load(i, h).wait()
+        store(i, h).start()
+    for i, h in pieces:
+        store(i, h).wait()
+
+
+def settle(arrays):
+    return pl.pallas_call(
+        settle_kernel,
+        in_specs=[pl.BlockSpec(memory_space=pl.ANY)] * 4,
+        out_specs=[pl.BlockSpec(memory_space=pl.ANY)] * 4,
+        out_shape=[jax.ShapeDtypeStruct(a.shape, a.dtype) for a in arrays],
+        scratch_shapes=[pltpu.VMEM(a.shape, a.dtype) for a in arrays]
+        + [pltpu.SemaphoreType.DMA((4, PARTS))] * 2,
+        compiler_params=pltpu.CompilerParams(vmem_limit_bytes=67043328),
+    )(*arrays)
+
+
 def per_device(query_proj, key_proj, value_proj, modality, out_weight, grad_projected):
     size, groups = lax.axis_size("ctx"), lax.axis_size("fsdp")
     rows, width = query_proj.shape[1:]
@@ -670,7 +706,7 @@
         grad_projected[0],
         modality,
     )
-    return tuple(a[None] for a in results)
+    return tuple(a[None] for a in settle(results))
 
 
 def aligned(mesh, query_shape, weight_shape):

time: 175 us -> 173 us (0.989)
  local copies, waits for them, and re-layouts: 6.15 us -> 0 us
  Pallas kernels: 166 us -> 170 us
    unnamed x10 -> x0, local copies, waits for them, and re-layouts: 6.15 us -> none
    pallas_call x0 -> x1, Pallas kernels: none -> 3.63 us  [settle(): pl.pallas_call(settle_kernel, in_specs=[pl.BlockSpec(memory_space=pl.ANY)...]
where the time goes in v3:
time: 173 us; the launch traced here: 170 us
  Pallas kernels  170 us (98%)
    pallas_call x1, Pallas kernels, per_device(): pl.pallas_call(functools.partial(middle_kernel, groups, size), in_specs=[...  166 us
    pallas_call x1, Pallas kernels, settle(): pl.pallas_call(settle_kernel, in_specs=[pl.BlockSpec(memory_space=pl.ANY)...  3.63 us

profile of v3, /device:TPU:8, one launch (start us, length us, event | category | flops | bytes accessed | tf_op | source)
XLA Modules:
  0.0 170.3 jit_solution(11509083191436985404)
XLA Ops:
  0.6 165.9 %shard_map.93 = (bf16[128,2048]{1,0:T(8,128)(2,1)}, bf16[128,4096]{1,0:T(8,128)(2,1)}, bf16[128,4096]{1,0:T(8,128)(2,1)}, bf16[128,4096]{1,0:T(8,128)(2,1)}) custom-call(bf16[128,4096]{1,0:T(8,128)(2,1)} %bitcast.9, bf16[128,4096]{1,0:T(8,128)(2,1)} %bitcast.10, bf16[128,4096]{1,0:T(8,128)(2,1)} %bitcast.11, bf16[256,2048]{1,0:T(8,128)(2,1)} %bitcast.12, ...), custom_call_target="tpu_custom_call" | custom-call | tf_op jit(solution)/shard_map/pallas_call | solution.py:670
  166.5 3.6 %shard_map.94 = (bf16[128,2048]{1,0:T(8,128)(2,1)}, bf16[128,4096]{1,0:T(8,128)(2,1)}, bf16[128,4096]{1,0:T(8,128)(2,1)}, bf16[128,4096]{1,0:T(8,128)(2,1)}) custom-call(bf16[128,2048]{1,0:T(8,128)(2,1)} %get-tuple-element.12.refs_0_, bf16[128,4096]{1,0:T(8,128)(2,1)} %get-tuple-element.13.refs_1_, bf16[128,4096]{1,0:T(8,128)(2,1)} %get-tuple-element.14.refs_2_, ...), custom_call_target="tpu_custom_call" | custom-call | tf_op jit(solution)/shard_map/pallas_call | solution.py:653

commit v4 on v3

--- a/solution.py
+++ b/solution.py
@@ -294,9 +294,6 @@
             sent(kvbuf.at[step, :, pl.ds(0, 3 * rows)], in_send.at[step])
 
     def compute(step, base, between=None):
-        both = lax.dot_general(up[...], wbuf[step], NT, preferred_element_type=jnp.float32)
-        image = marks[...] > 0.5
-        gbuf[...] = jnp.where(image, both[:, HEAD_SIZE:], both[:, :HEAD_SIZE]).astype(jnp.bfloat16)
         span = half // 2
         kept = []
         for block in range(2):
@@ -328,6 +325,9 @@
             )
         if between is not None:
             between()
+        both = lax.dot_general(up[...], wbuf[step], NT, preferred_element_type=jnp.float32)
+        image = marks[...] > 0.5
+        gbuf[...] = jnp.where(image, both[:, HEAD_SIZE:], both[:, :HEAD_SIZE]).astype(jnp.bfloat16)
         for block in reversed(range(2)):
             offset = block * span
             finish = base + offset + span

time: 173 us -> 174 us (level)
  no operation moved by 1% of the time
where the time goes in v4:
time: 174 us; the launch traced here: 171 us
  Pallas kernels  170 us (98%)
    pallas_call x1, Pallas kernels, per_device(): pl.pallas_call(functools.partial(middle_kernel, groups, size), in_specs=[...  167 us
    pallas_call x1, Pallas kernels, settle(): pl.pallas_call(settle_kernel, in_specs=[pl.BlockSpec(memory_space=pl.ANY)...  3.63 us

profile of v4, /device:TPU:8, one launch (start us, length us, event | category | flops | bytes accessed | tf_op | source)
XLA Modules:
  0.0 171.3 jit_solution(7178539912198800085)
XLA Ops:
  0.6 166.8 %shard_map.93 = (bf16[128,2048]{1,0:T(8,128)(2,1)}, bf16[128,4096]{1,0:T(8,128)(2,1)}, bf16[128,4096]{1,0:T(8,128)(2,1)}, bf16[128,4096]{1,0:T(8,128)(2,1)}) custom-call(bf16[128,4096]{1,0:T(8,128)(2,1)} %bitcast.9, bf16[128,4096]{1,0:T(8,128)(2,1)} %bitcast.10, bf16[128,4096]{1,0:T(8,128)(2,1)} %bitcast.11, bf16[256,2048]{1,0:T(8,128)(2,1)} %bitcast.12, ...), custom_call_target="tpu_custom_call" | custom-call | tf_op jit(solution)/shard_map/pallas_call | solution.py:670
  167.5 3.6 %shard_map.94 = (bf16[128,2048]{1,0:T(8,128)(2,1)}, bf16[128,4096]{1,0:T(8,128)(2,1)}, bf16[128,4096]{1,0:T(8,128)(2,1)}, bf16[128,4096]{1,0:T(8,128)(2,1)}) custom-call(bf16[128,2048]{1,0:T(8,128)(2,1)} %get-tuple-element.12.refs_0_, bf16[128,4096]{1,0:T(8,128)(2,1)} %get-tuple-element.13.refs_1_, bf16[128,4096]{1,0:T(8,128)(2,1)} %get-tuple-element.14.refs_2_, ...), custom_call_target="tpu_custom_call" | custom-call | tf_op jit(solution)/shard_map/pallas_call | solution.py:653
